TPU v7x, 256 devices: a whole 4x4x8 slice. The times are simulated.
256 devices in a mesh: blk: 8 (over y, core), wide: 32 (over x, z).
Axes of the slice: x: 4, y: 4, z: 8, core: 2. Of those that a mesh axis runs over, the one named last changes fastest.
Arguments:
- amplitudes: bfloat16 [2048, 262144], P(('blk', 'wide')), may hold values from -6 to 6
- integrals: bfloat16 [32, 256, 128, 128], P('wide', 'blk'), may hold values from -0.03125 to 0.03125
- out_tile: int32 [32, 256], P('wide'), may hold values from 0 to 31, as said below
- cd_slot: int32 [32, 256], P('wide'), may hold values from 0 to 63, as said below
Outputs:
- ladder: bfloat16 [2048, 4096], P('blk', 'wide')
Inputs may be any that keep to these rules, and one draw needn't show every extreme that they name: `out_tile`: output tile a lies in sector a mod 8. In each group every one of its 64 contracted tiles appears in exactly 4 entries, once with each output tile of one sector, the sector drawn for that tile; entries are in no particular order. `cd_slot`: see out_tile.
All inputs are finite; a program needn't handle non-finite values.
Results may differ from a plain program's by a relative error of at most 0.001.
Values may be sent and summed in bfloat16 or wider, within the bound.
No kernel may reach another device: no remote copies, remote signals or barrier semaphores. Data moves between devices by JAX's collectives and lax.ppermute only.
A program may use at most 192 MiB of HBM per device.

v0:
```python
import jax
import jax.numpy as jnp
from jax import lax
from jax.sharding import PartitionSpec as P

SECTORS = 8
A_PER = 4


def on_device(amplitudes, integrals, out_tile, cd_slot):
    n_out = SECTORS * A_PER
    tile_size = integrals.shape[2]
    exchanged = lax.all_to_all(amplitudes, "wide", split_axis=1, concat_axis=0, tiled=True)
    rows = exchanged.shape[0]
    columns = exchanged.reshape(rows, -1, tile_size)
    n_slots = columns.shape[1]
    outs_group = out_tile[0]
    slots_group = cd_slot[0]

    def accumulate(carry, piece, start):
        count = piece.shape[1]
        out_block = lax.dynamic_slice_in_dim(outs_group, start, count, 0)
        slot_block = lax.dynamic_slice_in_dim(slots_group, start, count, 0)
        slot_onehot = (slot_block[:, None] == jnp.arange(n_slots, dtype=jnp.int32)[None, :]).astype(
            jnp.bfloat16
        )
        picked = jnp.einsum(
            "kc,rct->rkt", slot_onehot, columns, preferred_element_type=jnp.float32
        ).astype(jnp.bfloat16)
        products = jnp.einsum("rkt,ktu->rku", picked, piece[0], preferred_element_type=jnp.float32)
        out_onehot = (out_block[:, None] == jnp.arange(n_out, dtype=jnp.int32)[None, :]).astype(
            jnp.float32
        )
        placed = jnp.einsum("ka,rku->rau", out_onehot, products, precision=lax.Precision.HIGHEST)
        return carry + placed

    empty = jnp.zeros((rows, n_out, tile_size), jnp.float32)
    everything = lax.all_gather(integrals, "blk", axis=1, tiled=True)
    count = integrals.shape[1]

    def step(index, carry):
        first = index * count
        piece = lax.dynamic_slice_in_dim(everything, first, count, 1)
        return accumulate(carry, piece, first)

    partial_sum = lax.fori_loop(0, lax.axis_size("blk"), step, empty)
    flat = partial_sum.reshape(rows, n_out * tile_size)
    return lax.psum_scatter(flat, "wide", scatter_dimension=1, tiled=True).astype(jnp.bfloat16)


def solution(mesh):
    in_specs = (
        P(("blk", "wide"), None),
        P("wide", "blk", None, None),
        P("wide", None),
        P("wide", None),
    )
    out_specs = P("blk", "wide")
    return jax.shard_map(
        on_device, mesh=mesh, in_specs=in_specs, out_specs=out_specs, check_vma=False
    )
```

profile of v0, /device:TPU:8, one launch (start us, length us, event | category | flops | bytes accessed | tf_op | source)
XLA Modules:
  0.0 524.1 jit_solution(3979197923908216875)
XLA Ops:
  6.5 0.0 all-gather.2.cloned.1.call-start
  6.5 0.7 all-gather.2.cloned.1.call-update
  7.3 11.5 %all-to-all-start = ((bf16[8,32,8192]{2,0,1:T(8,128)(2,1)}), bf16[8,32,8192]{2,0,1:T(8,128)(2,1)}, u32[]{:S(2)}, u32[]{:S(2)}) async-start(bf16[8,32,8192]{2,0,1:T(8,128)(2,1)} %bitcast.50), calls=%async_computation | async-start | bytes 8388608 | tf_op jit(solution)/shard_map/all_to_all | solution.py:13
  18.7 0.0 reduce-scatter.2.cloned.1.call-start
  18.8 96.9 %all-to-all-done = bf16[8,32,8192]{2,0,1:T(8,128)(2,1)} async-done(((bf16[8,32,8192]{2,0,1:T(8,128)(2,1)}), bf16[8,32,8192]{2,0,1:T(8,128)(2,1)}, u32[]{:S(2)}, u32[]{:S(2)}) %all-to-all-start) | async-done | bytes 4194336 | tf_op jit(solution)/shard_map/all_to_all | solution.py:13
  115.7 0.0 copy-start
  115.7 0.0 copy-start.1
  115.7 5.4 %copy.9 = bf16[32,8,64,128]{3,2,1,0:T(8,128)(2,1)} copy(bf16[32,8,64,128]{3,1,2,0:T(8,128)(2,1)} %bitcast.13) | data formatting | bytes 8388608
  121.1 0.0 all-gather.2.cloned.1.call-done
  121.1 0.0 copy-done
  121.1 0.0 copy-done.1
  121.1 165.7 %while.14 = (s32[]{:T(128)}, f32[256,32,128]{2,1,0:T(8,128)}, bf16[1,256,128,128]{3,2,1,0:T(8,128)(2,1)}, s32[256]{0:T(256)S(1)}, bf16[256,64,128]{2,1,0:T(8,128...) while((s32[]{:T(128)}, f32[256,32,128]{2,1,0:T(8,128)}, ...), condition=%wide.region_1.0_spmd.clone, body=%wide.region_0.0_spmd.clone.sunk | while | flops 807406592 | bytes 34603952 | solution.py:46
  121.1 0.1 dynamic_slice.33
  121.2 0.1 dynamic_slice.32
  121.3 2.9 fusion.32
  124.2 4.6 fusion.33
  128.8 5.5 %copy.20 = f32[32,128,256]{1,0,2:T(8,128)} copy(f32[32,128,256]{2,1,0:T(8,128)} %fusion.33) | data formatting | bytes 8388608 | tf_op jit(solution)/shard_map/while/body/eval_jaxpr/rkt,ktu->rku/dot_general | solution.py:30
  134.3 6.4 %bitcast_add_fusion.2 = f32[256,32,128]{2,1,0:T(8,128)} fusion(f32[256,32,128]{2,1,0:T(8,128)} %get-tuple-element.202, f32[32,128,256]{1,0,2:T(8,128)} %copy.20, pred[]{:T(512)S(6)} %compare.3, s32[32]{0:T(128)S(1)} %dynamic_slice.33), kind=kOutput, calls=%fused_computation.clone.1 | convolution fusion | flops 404751360 | bytes 12583041 | tf_op jit(solution)/shard_map/while/body/eval_jaxpr/ka,rku->rau/dot_general | solution.py:34
  140.7 0.1 dynamic_slice.33
  140.8 0.1 dynamic_slice.32
  140.9 2.9 fusion.32
  143.8 4.6 fusion.33
  148.4 5.5 %copy.20 = f32[32,128,256]{1,0,2:T(8,128)} copy(f32[32,128,256]{2,1,0:T(8,128)} %fusion.33) | data formatting | bytes 8388608 | tf_op jit(solution)/shard_map/while/body/eval_jaxpr/rkt,ktu->rku/dot_general | solution.py:30
  153.9 7.7 %bitcast_add_fusion.2 = f32[256,32,128]{2,1,0:T(8,128)} fusion(f32[256,32,128]{2,1,0:T(8,128)} %get-tuple-element.202, f32[32,128,256]{1,0,2:T(8,128)} %copy.20, pred[]{:T(512)S(6)} %compare.3, s32[32]{0:T(128)S(1)} %dynamic_slice.33), kind=kOutput, calls=%fused_computation.clone.1 | convolution fusion | flops 404751360 | bytes 12583041 | tf_op jit(solution)/shard_map/while/body/eval_jaxpr/ka,rku->rau/dot_general | solution.py:34
  161.6 0.1 dynamic_slice.33
  161.7 0.1 dynamic_slice.32
  161.7 2.9 fusion.32
  164.7 4.6 fusion.33
  169.3 5.5 %copy.20 = f32[32,128,256]{1,0,2:T(8,128)} copy(f32[32,128,256]{2,1,0:T(8,128)} %fusion.33) | data formatting | bytes 8388608 | tf_op jit(solution)/shard_map/while/body/eval_jaxpr/rkt,ktu->rku/dot_general | solution.py:30
  174.7 7.7 %bitcast_add_fusion.2 = f32[256,32,128]{2,1,0:T(8,128)} fusion(f32[256,32,128]{2,1,0:T(8,128)} %get-tuple-element.202, f32[32,128,256]{1,0,2:T(8,128)} %copy.20, pred[]{:T(512)S(6)} %compare.3, s32[32]{0:T(128)S(1)} %dynamic_slice.33), kind=kOutput, calls=%fused_computation.clone.1 | convolution fusion | flops 404751360 | bytes 12583041 | tf_op jit(solution)/shard_map/while/body/eval_jaxpr/ka,rku->rau/dot_general | solution.py:34
  182.5 0.1 dynamic_slice.33
  182.5 0.1 dynamic_slice.32
  182.6 2.9 fusion.32
  185.5 4.6 fusion.33
  190.1 5.5 %copy.20 = f32[32,128,256]{1,0,2:T(8,128)} copy(f32[32,128,256]{2,1,0:T(8,128)} %fusion.33) | data formatting | bytes 8388608 | tf_op jit(solution)/shard_map/while/body/eval_jaxpr/rkt,ktu->rku/dot_general | solution.py:30
  195.6 7.7 %bitcast_add_fusion.2 = f32[256,32,128]{2,1,0:T(8,128)} fusion(f32[256,32,128]{2,1,0:T(8,128)} %get-tuple-element.202, f32[32,128,256]{1,0,2:T(8,128)} %copy.20, pred[]{:T(512)S(6)} %compare.3, s32[32]{0:T(128)S(1)} %dynamic_slice.33), kind=kOutput, calls=%fused_computation.clone.1 | convolution fusion | flops 404751360 | bytes 12583041 | tf_op jit(solution)/shard_map/while/body/eval_jaxpr/ka,rku->rau/dot_general | solution.py:34
  203.3 0.1 dynamic_slice.33
  203.4 0.1 dynamic_slice.32
  203.5 2.9 fusion.32
  206.4 4.6 fusion.33
  211.0 5.5 %copy.20 = f32[32,128,256]{1,0,2:T(8,128)} copy(f32[32,128,256]{2,1,0:T(8,128)} %fusion.33) | data formatting | bytes 8388608 | tf_op jit(solution)/shard_map/while/body/eval_jaxpr/rkt,ktu->rku/dot_general | solution.py:30
  216.5 7.7 %bitcast_add_fusion.2 = f32[256,32,128]{2,1,0:T(8,128)} fusion(f32[256,32,128]{2,1,0:T(8,128)} %get-tuple-element.202, f32[32,128,256]{1,0,2:T(8,128)} %copy.20, pred[]{:T(512)S(6)} %compare.3, s32[32]{0:T(128)S(1)} %dynamic_slice.33), kind=kOutput, calls=%fused_computation.clone.1 | convolution fusion | flops 404751360 | bytes 12583041 | tf_op jit(solution)/shard_map/while/body/eval_jaxpr/ka,rku->rau/dot_general | solution.py:34
  224.2 0.1 dynamic_slice.33
  224.3 0.1 dynamic_slice.32
  224.3 2.9 fusion.32
  227.3 4.6 fusion.33
  231.9 5.5 %copy.20 = f32[32,128,256]{1,0,2:T(8,128)} copy(f32[32,128,256]{2,1,0:T(8,128)} %fusion.33) | data formatting | bytes 8388608 | tf_op jit(solution)/shard_map/while/body/eval_jaxpr/rkt,ktu->rku/dot_general | solution.py:30
  237.3 7.7 %bitcast_add_fusion.2 = f32[256,32,128]{2,1,0:T(8,128)} fusion(f32[256,32,128]{2,1,0:T(8,128)} %get-tuple-element.202, f32[32,128,256]{1,0,2:T(8,128)} %copy.20, pred[]{:T(512)S(6)} %compare.3, s32[32]{0:T(128)S(1)} %dynamic_slice.33), kind=kOutput, calls=%fused_computation.clone.1 | convolution fusion | flops 404751360 | bytes 12583041 | tf_op jit(solution)/shard_map/while/body/eval_jaxpr/ka,rku->rau/dot_general | solution.py:34
  245.1 0.1 dynamic_slice.33
  245.1 0.1 dynamic_slice.32
  245.2 2.9 fusion.32
  248.2 4.6 fusion.33
  252.7 5.5 %copy.20 = f32[32,128,256]{1,0,2:T(8,128)} copy(f32[32,128,256]{2,1,0:T(8,128)} %fusion.33) | data formatting | bytes 8388608 | tf_op jit(solution)/shard_map/while/body/eval_jaxpr/rkt,ktu->rku/dot_general | solution.py:30
  258.2 7.7 %bitcast_add_fusion.2 = f32[256,32,128]{2,1,0:T(8,128)} fusion(f32[256,32,128]{2,1,0:T(8,128)} %get-tuple-element.202, f32[32,128,256]{1,0,2:T(8,128)} %copy.20, pred[]{:T(512)S(6)} %compare.3, s32[32]{0:T(128)S(1)} %dynamic_slice.33), kind=kOutput, calls=%fused_computation.clone.1 | convolution fusion | flops 404751360 | bytes 12583041 | tf_op jit(solution)/shard_map/while/body/eval_jaxpr/ka,rku->rau/dot_general | solution.py:34
  265.9 0.1 dynamic_slice.33
  266.0 0.1 dynamic_slice.32
  266.1 2.9 fusion.32
  269.0 4.6 fusion.33
  273.6 5.5 %copy.20 = f32[32,128,256]{1,0,2:T(8,128)} copy(f32[32,128,256]{2,1,0:T(8,128)} %fusion.33) | data formatting | bytes 8388608 | tf_op jit(solution)/shard_map/while/body/eval_jaxpr/rkt,ktu->rku/dot_general | solution.py:30
  279.1 7.7 %bitcast_add_fusion.2 = f32[256,32,128]{2,1,0:T(8,128)} fusion(f32[256,32,128]{2,1,0:T(8,128)} %get-tuple-element.202, f32[32,128,256]{1,0,2:T(8,128)} %copy.20, pred[]{:T(512)S(6)} %compare.3, s32[32]{0:T(128)S(1)} %dynamic_slice.33), kind=kOutput, calls=%fused_computation.clone.1 | convolution fusion | flops 404751360 | bytes 12583041 | tf_op jit(solution)/shard_map/while/body/eval_jaxpr/ka,rku->rau/dot_general | solution.py:34
  286.8 7.9 %copy.16 = f32[32,8,32,128]{3,1,2,0:T(8,128)} copy(f32[32,8,32,128]{3,2,1,0:T(8,128)} %bitcast.47) | data formatting | bytes 8388608
  294.7 0.0 reduce-scatter.2.cloned.1.call-update
  294.7 221.0 %reduce-scatter.2.cloned.1.call-done = f32[256,128]{1,0:T(8,128)} async-done(((f32[256,4096]{1,0:T(8,128)}), f32[256,128]{1,0:T(8,128)}) %reduce-scatter.2.cloned.1.call-update) | async-done | bytes 131088 | tf_op jit(solution)/shard_map/reduce_scatter | solution.py:48
  515.7 1.5 convert_element_type.19
  (1 shorter events, 0.0 us)
Async XLA Ops:
  6.5 114.6 %all-gather.2.cloned.1.call-start = ((), (), s32[]{:S(2)}) async-start(), calls=%async_computation.2 | async-start | bytes 9437184 | tf_op jit(solution)/shard_map/all_gather | solution.py:38
  7.3 108.5 %all-to-all-start = ((bf16[8,32,8192]{2,0,1:T(8,128)(2,1)}), bf16[8,32,8192]{2,0,1:T(8,128)(2,1)}, u32[]{:S(2)}, u32[]{:S(2)}) async-start(bf16[8,32,8192]{2,0,1:T(8,128)(2,1)} %bitcast.50), calls=%async_computation | async-start | bytes 8388608 | tf_op jit(solution)/shard_map/all_to_all | solution.py:13
  18.7 497.0 %reduce-scatter.2.cloned.1.call-start = ((), (), s32[]{:S(2)}) async-start(), calls=%async_computation.3 | async-start | bytes 4325376 | tf_op jit(solution)/shard_map/reduce_scatter | solution.py:48
  115.7 5.4 %copy-start = (s32[1,256]{1,0:T(1,128)S(1)}, s32[1,256]{1,0:T(1,128)}, u32[]{:S(2)}) copy-start(s32[1,256]{1,0:T(1,128)} %param.9) | copy-start | bytes 3076
  115.7 5.4 %copy-start.1 = (s32[1,256]{1,0:T(1,128)S(1)}, s32[1,256]{1,0:T(1,128)}, u32[]{:S(2)}) copy-start(s32[1,256]{1,0:T(1,128)} %param.8) | copy-start | bytes 3076
Sparse Core Ops, SparseCore 0:
  9.2 54.2 all-gather.1
  294.8 220.8 reduce-scatter.1
where the time goes:
time: 526 us; the launch traced here: 524 us
  waiting for transfers between devices  319 us (61%)
  matrix products  121 us (23%)
  local copies, waits for them, and re-layouts  58.2 us (11%)
  between operations  13.4 us (3%)
  starting transfers between devices  11.5 us (2%)
    reduce_scatter x1, waiting for transfers between devices, on_device(): lax.psum_scatter(flat, 'wide', scatter_dimension=1, tiled=True)  221 us
    all_to_all x1, waiting for transfers between devices, on_device(): lax.all_to_all(amplitudes, 'wide', split_axis=1, concat_axis=0, tiled=True)  96.9 us
    dot_general x8, matrix products, accumulate(): jnp.einsum('ka,rku->rau', out_onehot, products, precision=lax.Precision.H...  60.4 us
    dot_general x8, local copies, waits for them, and re-layouts, accumulate(): jnp.einsum('rkt,ktu->rku', picked, piece[0], preferred_element_type=jnp.f...  43.7 us
    dot_general x8, matrix products, accumulate(): jnp.einsum('rkt,ktu->rku', picked, piece[0], preferred_element_type=jnp.f...  36.7 us
    dot_general x8, matrix products, accumulate(): jnp.einsum('kc,rct->rkt', slot_onehot, columns, preferred_element_type=jn...  23.5 us
    unnamed x6, local copies, waits for them, and re-layouts  13.3 us
    all_to_all x1, starting transfers between devices, on_device(): lax.all_to_all(amplitudes, 'wide', split_axis=1, concat_axis=0, tiled=True)  11.5 us
  transfers between devices with their start and end apart: 3, of which 2 were waited for; matrix products, arithmetic and copies ran while one was open for 1% of the time, Pallas kernels for 0%

commit v1 on v0

--- a/solution.py
+++ b/solution.py
@@ -10,7 +10,12 @@
 def on_device(amplitudes, integrals, out_tile, cd_slot):
     n_out = SECTORS * A_PER
     tile_size = integrals.shape[2]
-    exchanged = lax.all_to_all(amplitudes, "wide", split_axis=1, concat_axis=0, tiled=True)
+    exchanged = jnp.concatenate(
+        lax.all_to_all(
+            jnp.stack(jnp.split(amplitudes, lax.axis_size("wide"), axis=1)), "wide", 0, 0
+        ),
+        axis=0,
+    )
     rows = exchanged.shape[0]
     columns = exchanged.reshape(rows, -1, tile_size)
     n_slots = columns.shape[1]

time: 526 us -> 577 us (1.097)
  local copies, waits for them, and re-layouts: 58.2 us -> 108 us
    unnamed x6 -> x37, local copies, waits for them, and re-layouts: 13.3 us -> 62 us
  transfers between devices with their start and end apart: 3 -> 3, of which waited for: 2 -> 2; matrix products, arithmetic and copies ran while one was open for 1% -> 10% of each run, Pallas kernels for 0% -> 0%
where the time goes in v1:
time: 577 us; the launch traced here: 574 us
  waiting for transfers between devices  319 us (55%)
  matrix products  121 us (21%)
  local copies, waits for them, and re-layouts  108 us (19%)
  between operations  13.4 us (2%)
  starting transfers between devices  11.5 us (2%)
    reduce_scatter x1, waiting for transfers between devices, on_device(): lax.psum_scatter(flat, 'wide', scatter_dimension=1, tiled=True)  221 us
    all_to_all x1, waiting for transfers between devices, on_device(): lax.all_to_all(jnp.stack(jnp.split(amplitudes, lax.axis_size('wide'), axi...  97 us
    unnamed x37, local copies, waits for them, and re-layouts  62 us
    dot_general x8, matrix products, accumulate(): jnp.einsum('ka,rku->rau', out_onehot, products, precision=lax.Precision.H...  60.4 us
    dot_general x8, local copies, waits for them, and re-layouts, accumulate(): jnp.einsum('rkt,ktu->rku', picked, piece[0], preferred_element_type=jnp.f...  43.7 us
    dot_general x8, matrix products, accumulate(): jnp.einsum('rkt,ktu->rku', picked, piece[0], preferred_element_type=jnp.f...  36.7 us
    dot_general x8, matrix products, accumulate(): jnp.einsum('kc,rct->rkt', slot_onehot, columns, preferred_element_type=jn...  23.5 us
  transfers between devices with their start and end apart: 3, of which 2 were waited for; matrix products, arithmetic and copies ran while one was open for 10% of the time, Pallas kernels for 0%

profile of v1, /device:TPU:8, one launch (start us, length us, event | category | flops | bytes accessed | tf_op | source)
XLA Modules:
  0.0 574.5 jit_solution(13439096934357297630)
XLA Ops:
  7.3 1.6 bitcast_dynamic-update-slice_fusion.31
  10.4 1.6 bitcast_dynamic-update-slice_fusion.29
  15.1 1.6 bitcast_dynamic-update-slice_fusion.26
  16.7 1.6 bitcast_dynamic-update-slice_fusion.25
  18.2 1.6 bitcast_dynamic-update-slice_fusion.24
  19.8 1.6 bitcast_dynamic-update-slice_fusion.23
  21.4 1.6 bitcast_dynamic-update-slice_fusion.22
  22.9 1.6 bitcast_dynamic-update-slice_fusion.21
  24.5 1.6 bitcast_dynamic-update-slice_fusion.20
  26.1 1.6 bitcast_dynamic-update-slice_fusion.19
  27.7 1.6 bitcast_dynamic-update-slice_fusion.18
  29.3 1.6 bitcast_dynamic-update-slice_fusion.17
  30.8 1.6 bitcast_dynamic-update-slice_fusion.16
  32.4 1.6 bitcast_dynamic-update-slice_fusion.15
  34.0 1.6 bitcast_dynamic-update-slice_fusion.14
  35.6 1.6 bitcast_dynamic-update-slice_fusion.13
  37.2 1.6 bitcast_dynamic-update-slice_fusion.12
  38.7 1.6 bitcast_dynamic-update-slice_fusion.11
  40.3 1.6 bitcast_dynamic-update-slice_fusion.10
  41.9 1.6 bitcast_dynamic-update-slice_fusion.9
  46.6 1.6 bitcast_dynamic-update-slice_fusion.6
  48.1 1.6 bitcast_dynamic-update-slice_fusion.5
  49.7 1.6 bitcast_dynamic-update-slice_fusion.4
  51.3 1.6 bitcast_dynamic-update-slice_fusion.3
  54.4 1.6 bitcast_dynamic-update-slice_fusion.1
  55.9 1.6 bitcast_dynamic-update-slice_fusion
  57.5 11.5 %all-to-all-start = ((bf16[32,8,8192]{2,1,0:T(8,128)(2,1)}), bf16[32,8,8192]{2,1,0:T(8,128)(2,1)}, u32[]{:S(2)}, u32[]{:S(2)}) async-start(bf16[32,8,8192]{2,1,0:T(8,128)(2,1)} %bitcast_dynamic-update-slice_fusion), calls=%async_computation | async-start | bytes 8388608 | tf_op jit(solution)/shard_map/all_to_all | solution.py:14
  69.1 97.0 %all-to-all-done = bf16[32,8,8192]{2,1,0:T(8,128)(2,1)} async-done(((bf16[32,8,8192]{2,1,0:T(8,128)(2,1)}), bf16[32,8,8192]{2,1,0:T(8,128)(2,1)}, u32[]{:S(2)}, u32[]{:S(2)}) %all-to-all-start) | async-done | bytes 4194336 | tf_op jit(solution)/shard_map/all_to_all | solution.py:14
  166.1 5.4 copy.9
  171.5 165.7 %while.14 = (s32[]{:T(128)}, f32[256,32,128]{2,1,0:T(8,128)}, bf16[1,256,128,128]{3,2,1,0:T(8,128)(2,1)}, s32[256]{0:T(256)S(1)}, bf16[256,64,128]{2,1,0:T(8,128...) while((s32[]{:T(128)}, f32[256,32,128]{2,1,0:T(8,128)}, ...), condition=%wide.region_1.0_spmd.clone, body=%wide.region_0.0_spmd.clone.sunk | while | flops 807406592 | bytes 34603952 | solution.py:51
  171.7 2.9 fusion.32
  174.6 4.6 fusion.33
  179.2 5.5 copy.20
  184.7 6.4 %bitcast_add_fusion.2 = f32[256,32,128]{2,1,0:T(8,128)} fusion(f32[256,32,128]{2,1,0:T(8,128)} %get-tuple-element.202, f32[32,128,256]{1,0,2:T(8,128)} %copy.20, pred[]{:T(512)S(6)} %compare.3, s32[32]{0:T(128)S(1)} %dynamic_slice.33), kind=kOutput, calls=%fused_computation.clone.1 | convolution fusion | flops 404751360 | bytes 12583041 | tf_op jit(solution)/shard_map/while/body/eval_jaxpr/ka,rku->rau/dot_general | solution.py:39
  191.3 2.9 fusion.32
  194.2 4.6 fusion.33
  198.8 5.5 copy.20
  204.3 7.7 %bitcast_add_fusion.2 = f32[256,32,128]{2,1,0:T(8,128)} fusion(f32[256,32,128]{2,1,0:T(8,128)} %get-tuple-element.202, f32[32,128,256]{1,0,2:T(8,128)} %copy.20, pred[]{:T(512)S(6)} %compare.3, s32[32]{0:T(128)S(1)} %dynamic_slice.33), kind=kOutput, calls=%fused_computation.clone.1 | convolution fusion | flops 404751360 | bytes 12583041 | tf_op jit(solution)/shard_map/while/body/eval_jaxpr/ka,rku->rau/dot_general | solution.py:39
  212.1 2.9 fusion.32
  215.1 4.6 fusion.33
  219.7 5.5 copy.20
  225.1 7.7 %bitcast_add_fusion.2 = f32[256,32,128]{2,1,0:T(8,128)} fusion(f32[256,32,128]{2,1,0:T(8,128)} %get-tuple-element.202, f32[32,128,256]{1,0,2:T(8,128)} %copy.20, pred[]{:T(512)S(6)} %compare.3, s32[32]{0:T(128)S(1)} %dynamic_slice.33), kind=kOutput, calls=%fused_computation.clone.1 | convolution fusion | flops 404751360 | bytes 12583041 | tf_op jit(solution)/shard_map/while/body/eval_jaxpr/ka,rku->rau/dot_general | solution.py:39
  233.0 2.9 fusion.32
  236.0 4.6 fusion.33
  240.5 5.5 copy.20
  246.0 7.7 %bitcast_add_fusion.2 = f32[256,32,128]{2,1,0:T(8,128)} fusion(f32[256,32,128]{2,1,0:T(8,128)} %get-tuple-element.202, f32[32,128,256]{1,0,2:T(8,128)} %copy.20, pred[]{:T(512)S(6)} %compare.3, s32[32]{0:T(128)S(1)} %dynamic_slice.33), kind=kOutput, calls=%fused_computation.clone.1 | convolution fusion | flops 404751360 | bytes 12583041 | tf_op jit(solution)/shard_map/while/body/eval_jaxpr/ka,rku->rau/dot_general | solution.py:39
  253.9 2.9 fusion.32
  256.8 4.6 fusion.33
  261.4 5.5 copy.20
  266.9 7.7 %bitcast_add_fusion.2 = f32[256,32,128]{2,1,0:T(8,128)} fusion(f32[256,32,128]{2,1,0:T(8,128)} %get-tuple-element.202, f32[32,128,256]{1,0,2:T(8,128)} %copy.20, pred[]{:T(512)S(6)} %compare.3, s32[32]{0:T(128)S(1)} %dynamic_slice.33), kind=kOutput, calls=%fused_computation.clone.1 | convolution fusion | flops 404751360 | bytes 12583041 | tf_op jit(solution)/shard_map/while/body/eval_jaxpr/ka,rku->rau/dot_general | solution.py:39
  274.7 2.9 fusion.32
  277.7 4.6 fusion.33
  282.3 5.5 copy.20
  287.7 7.7 %bitcast_add_fusion.2 = f32[256,32,128]{2,1,0:T(8,128)} fusion(f32[256,32,128]{2,1,0:T(8,128)} %get-tuple-element.202, f32[32,128,256]{1,0,2:T(8,128)} %copy.20, pred[]{:T(512)S(6)} %compare.3, s32[32]{0:T(128)S(1)} %dynamic_slice.33), kind=kOutput, calls=%fused_computation.clone.1 | convolution fusion | flops 404751360 | bytes 12583041 | tf_op jit(solution)/shard_map/while/body/eval_jaxpr/ka,rku->rau/dot_general | solution.py:39
  295.6 2.9 fusion.32
  298.6 4.6 fusion.33
  303.1 5.5 copy.20
  308.6 7.7 %bitcast_add_fusion.2 = f32[256,32,128]{2,1,0:T(8,128)} fusion(f32[256,32,128]{2,1,0:T(8,128)} %get-tuple-element.202, f32[32,128,256]{1,0,2:T(8,128)} %copy.20, pred[]{:T(512)S(6)} %compare.3, s32[32]{0:T(128)S(1)} %dynamic_slice.33), kind=kOutput, calls=%fused_computation.clone.1 | convolution fusion | flops 404751360 | bytes 12583041 | tf_op jit(solution)/shard_map/while/body/eval_jaxpr/ka,rku->rau/dot_general | solution.py:39
  316.5 2.9 fusion.32
  319.4 4.6 fusion.33
  324.0 5.5 copy.20
  329.5 7.7 %bitcast_add_fusion.2 = f32[256,32,128]{2,1,0:T(8,128)} fusion(f32[256,32,128]{2,1,0:T(8,128)} %get-tuple-element.202, f32[32,128,256]{1,0,2:T(8,128)} %copy.20, pred[]{:T(512)S(6)} %compare.3, s32[32]{0:T(128)S(1)} %dynamic_slice.33), kind=kOutput, calls=%fused_computation.clone.1 | convolution fusion | flops 404751360 | bytes 12583041 | tf_op jit(solution)/shard_map/while/body/eval_jaxpr/ka,rku->rau/dot_general | solution.py:39
  337.2 7.9 %copy.16 = f32[32,8,32,128]{3,1,2,0:T(8,128)} copy(f32[32,8,32,128]{3,2,1,0:T(8,128)} %bitcast.109) | data formatting | bytes 8388608
  345.1 221.0 %reduce-scatter.2.cloned.1.call-done = f32[256,128]{1,0:T(8,128)} async-done(((f32[256,4096]{1,0:T(8,128)}), f32[256,128]{1,0:T(8,128)}) %reduce-scatter.2.cloned.1.call-update) | async-done | bytes 131088 | tf_op jit(solution)/shard_map/reduce_scatter | solution.py:53
  (33 shorter events, 12.9 us)
Async XLA Ops:
  6.5 165.0 %all-gather.2.cloned.1.call-start = ((), (), s32[]{:S(2)}) async-start(), calls=%async_computation.2 | async-start | bytes 9437184 | tf_op jit(solution)/shard_map/all_gather | solution.py:43
  57.5 108.6 %all-to-all-start = ((bf16[32,8,8192]{2,1,0:T(8,128)(2,1)}), bf16[32,8,8192]{2,1,0:T(8,128)(2,1)}, u32[]{:S(2)}, u32[]{:S(2)}) async-start(bf16[32,8,8192]{2,1,0:T(8,128)(2,1)} %bitcast_dynamic-update-slice_fusion), calls=%async_computation | async-start | bytes 8388608 | tf_op jit(solution)/shard_map/all_to_all | solution.py:14
  69.0 497.1 %reduce-scatter.2.cloned.1.call-start = ((), (), s32[]{:S(2)}) async-start(), calls=%async_computation.3 | async-start | bytes 4325376 | tf_op jit(solution)/shard_map/reduce_scatter | solution.py:53
  166.1 5.4 copy-start
  166.1 5.4 copy-start.1
Sparse Core Ops, SparseCore 0:
  9.2 54.2 all-gather.1
  345.3 220.7 reduce-scatter.1
